TPU v7x, 512 devices: a whole 4x4x16 slice. The times are simulated.
512 devices in a mesh: col: 64 (over y, x, z_lo), row: 8 (over z_hi, core).
Axes of the slice: x: 4, y: 4, z: 16 (z_hi: 4, z_lo: 4; z = z_hi * 4 + z_lo), core: 2. Of those that a mesh axis runs over, the one named last changes fastest.
Arguments:
- slab_embed: float32 [64, 4096], P(None, 'row'), may hold values from -6 to 6
- slab_probe: float32 [32, 4096], P(None, 'row'), may hold values from -6 to 6
- point_embed: float32 [64, 131072], P(None, 'col'), may hold values from -6 to 6
- point_probe: float32 [32, 131072], P(None, 'col'), may hold values from -1.2 to 1.2
- inv_scale: float32 [64], replicated, may hold values from 0.08 to 0.3
Outputs:
- slab_grad: float32 [64, 4096], P(None, 'row')
- point_grad: float32 [64, 131072], P(None, 'col')
All inputs are finite; a program needn't handle non-finite values.
Results may differ from a plain program's by a relative error of at most 0.0001.
Values sent between devices are 32-bit elements; how exact they have to be, the bound alone decides.
A program may use at most 64 MiB of HBM per device.

v0:
```python
import jax
import jax.numpy as jnp
from jax import lax
from jax.sharding import PartitionSpec as P


def local(slab_embed, slab_probe, point_embed, point_probe, inv_scale):
    hp = lax.Precision.HIGHEST
    weight_sq = inv_scale * inv_scale
    scaled = slab_embed * weight_sq[:, None]
    self_term = jnp.sum(scaled * slab_embed, axis=0)
    points_here = point_embed.shape[1]
    width = min(1024, points_here)
    row_total = jnp.zeros((slab_embed.shape[1],), jnp.float32)
    mixed = jnp.zeros(slab_embed.shape, jnp.float32)
    pieces = []
    for block in range(points_here // width):
        points = point_embed[:, block * width : (block + 1) * width]
        probes = point_probe[:, block * width : (block + 1) * width]
        other_term = jnp.sum(weight_sq[:, None] * points * points, axis=0)
        cross = jnp.dot(scaled.T, points, precision=hp)
        kernel = jnp.exp(-0.5 * (self_term[:, None] + other_term[None, :] - 2.0 * cross))
        weights = kernel * jnp.dot(slab_probe.T, probes, precision=hp)
        row_total = row_total + jnp.sum(weights, axis=1)
        mixed = mixed + jnp.dot(points, weights.T, precision=hp)
        pieces.append(
            weight_sq[:, None]
            * (
                jnp.dot(slab_embed, weights, precision=hp)
                - points * jnp.sum(weights, axis=0)[None, :]
            )
        )
    slab_terms = -weight_sq[:, None] * (slab_embed * row_total[None, :] - mixed)
    point_terms = jnp.concatenate(pieces, axis=1)
    slab_grad = lax.psum(slab_terms, "col")
    point_grad = lax.psum(point_terms, "row")
    return (slab_grad, point_grad)


def solution(mesh):
    placed = (P(None, "row"), P(None, "row"), P(None, "col"), P(None, "col"), P())
    return jax.shard_map(
        local,
        mesh=mesh,
        in_specs=placed,
        out_specs=(P(None, "row"), P(None, "col")),
        check_vma=False,
    )
```

profile of v0, /device:TPU:1, one launch (start us, length us, event | category | flops | bytes accessed | tf_op | source)
XLA Modules:
  0.0 783.1 jit_solution(10574615676581666491)
XLA Ops:
  7.2 0.0 copy-start
  7.2 0.0 copy-start.4
  7.2 0.0 copy-start.3
  7.2 0.0 all-reduce.3.cloned.1.call-start
  7.2 0.7 multiply_negate_fusion
  8.0 1.0 fusion.18
  9.0 1.2 fusion.8
  10.2 0.0 copy-start.5
  10.2 3.0 fusion.14
  13.2 0.0 copy-done.4
  13.2 0.0 copy-done.3
  13.2 1.9 fusion.10
  15.1 0.0 copy-done
  15.1 0.0 copy-done.5
  15.1 2.4 fusion.23
  17.5 2.2 fusion.12
  19.6 2.4 fusion.24
  22.0 0.0 copy-start.1
  22.1 1.3 copy-done.1
  23.4 2.8 fusion.6
  26.2 0.0 all-reduce.3.cloned.1.call-update
  26.2 0.2 all-reduce.5.cloned.1.call-start
  26.5 0.0 copy-start.2
  26.5 1.5 fusion.3
  27.9 0.1 copy-done.2
  28.1 1.5 fusion.1
  29.5 0.8 pad_maximum_fusion
  30.3 0.0 all-reduce.5.cloned.1.call-update
  30.4 622.6 %all-reduce.3.cloned.1.call-done = f32[64,512]{1,0:T(8,128)} async-done(((f32[64,512]{1,0:T(8,128)}), f32[64,512]{1,0:T(8,128)}) %all-reduce.3.cloned.1.call-update) | async-done | bytes 131088 | tf_op jit(solution)/shard_map/psum | solution.py:35
  652.9 119.9 %all-reduce.5.cloned.1.call-done = f32[64,2048]{1,0:T(8,128)} async-done(((f32[64,2048]{1,0:T(8,128)}), f32[64,2048]{1,0:T(8,128)}) %all-reduce.5.cloned.1.call-update) | async-done | bytes 524304 | tf_op jit(solution)/shard_map/psum | solution.py:36
  772.8 1.6 copy.9
  774.4 1.9 copy.10
  (1 shorter events, 0.0 us)
Async XLA Ops:
  7.2 7.9 %copy-start = (f32[32,512]{1,0:T(8,128)S(1)}, f32[32,512]{1,0:T(8,128)}, u32[]{:S(2)}) copy-start(f32[32,512]{1,0:T(8,128)} %param.6) | copy-start | bytes 196612
  7.2 6.0 copy-start.4
  7.2 6.0 copy-start.3
  7.2 645.7 %all-reduce.3.cloned.1.call-start = ((), (), s32[]{:S(2)}) async-start(), calls=%async_computation | async-start | bytes 262144 | tf_op jit(solution)/shard_map/psum | solution.py:35
  10.2 4.9 copy-start.5
  22.0 1.4 copy-start.1
  26.2 746.6 %all-reduce.5.cloned.1.call-start = ((), (), s32[]{:S(2)}) async-start(), calls=%async_computation.1 | async-start | bytes 1048576 | tf_op jit(solution)/shard_map/psum | solution.py:36
  26.5 1.6 copy-start.2
Sparse Core Ops, SparseCore 0:
  26.4 626.5 all-reduce.2
  656.7 116.1 all-reduce.4
where the time goes:
time: 783 us
  waiting for transfers between devices  743 us (95%)
  matrix products  17.5 us (2%)
  between operations  14.1 us (2%)
    psum x1, waiting for transfers between devices, local(): slab_grad = lax.psum(slab_terms, 'col')  623 us
    psum x1, waiting for transfers between devices, local(): point_grad = lax.psum(point_terms, 'row')  120 us
  transfers between devices with their start and end apart: 2, of which 2 were waited for; matrix products, arithmetic and copies ran while one was open for 0% of the time, Pallas kernels for 0%

commit v1 on v0

--- a/solution.py
+++ b/solution.py
@@ -32,7 +32,7 @@
         )
     slab_terms = -weight_sq[:, None] * (slab_embed * row_total[None, :] - mixed)
     point_terms = jnp.concatenate(pieces, axis=1)
-    slab_grad = lax.psum(slab_terms, "col")
+    slab_grad = jnp.sum(lax.all_gather(slab_terms, "col"), axis=0)
     point_grad = lax.psum(point_terms, "row")
     return (slab_grad, point_grad)
 

time: 783 us -> 430 us (0.55)
  the two profiles are of different devices: /device:TPU:1 before, /device:TPU:128 now
where the time goes in v1:
time: 430 us
  waiting for transfers between devices  385 us (90%)
  matrix products  17.5 us (4%)
  between operations  15.6 us (4%)
  other arithmetic  8.47 us (2%)
    all_gather x1, waiting for transfers between devices, local(): slab_grad = jnp.sum(lax.all_gather(slab_terms, 'col'), axis=0)  385 us
  transfers between devices with their start and end apart: 2, of which 1 were waited for; matrix products, arithmetic and copies ran while one was open for 2% of the time, Pallas kernels for 0%

profile of v1, /device:TPU:128, one launch (start us, length us, event | category | flops | bytes accessed | tf_op | source)
XLA Modules:
  0.0 430.1 jit_solution(4431955149218937922)
XLA Ops:
  8.0 0.0 copy-start
  8.0 0.0 copy-start.4
  8.0 0.0 copy-start.3
  8.0 0.0 all-gather.3.cloned.1.call-start
  8.1 0.7 multiply_negate_fusion
  8.8 1.0 fusion.18
  9.8 1.2 fusion.8
  11.0 0.0 copy-start.5
  11.0 3.0 fusion.14
  14.0 0.0 copy-done.4
  14.0 0.0 copy-done.3
  14.0 1.9 fusion.10
  15.9 0.0 copy-done
  15.9 0.0 copy-done.5
  15.9 2.4 fusion.23
  18.3 2.2 fusion.12
  20.5 2.4 fusion.24
  22.9 0.0 copy-start.1
  22.9 1.4 copy-done.1
  24.3 2.8 fusion.6
  27.1 0.0 all-gather.3.cloned.1.call-update
  27.1 0.2 all-reduce.2.cloned.1.call-start
  27.3 0.0 copy-start.2
  27.3 1.5 fusion.3
  28.8 0.1 copy-done.2
  28.9 1.5 fusion.1
  30.4 0.8 pad_maximum_fusion
  31.2 0.0 all-reduce.2.cloned.1.call-update
  31.2 384.8 %all-gather.3.cloned.1.call-done = f32[4096,512]{1,0:T(8,128)} async-done(((f32[64,512]{1,0:T(8,128)}), f32[4096,512]{1,0:T(8,128)}) %all-gather.3.cloned.1.call-update) | async-done | bytes 8388624 | tf_op jit(solution)/shard_map/all_gather | solution.py:35
  416.0 4.7 %reduce_sum.77 = f32[64,512]{1,0:T(8,128)} reduce(f32[64,64,512]{2,1,0:T(8,128)} %bitcast.27, f32[]{:T(128)} %constant.0.clone.1), dimensions={0}, to_apply=%region_5.0 | reduce | flops 2064384 | bytes 8519684 | tf_op jit(solution)/shard_map/reduce_sum | solution.py:35
  420.8 0.0 all-reduce.2.cloned.1.call-done
  420.8 1.9 copy.8
  (1 shorter events, 0.0 us)
Async XLA Ops:
  8.0 7.9 %copy-start = (f32[32,512]{1,0:T(8,128)S(1)}, f32[32,512]{1,0:T(8,128)}, u32[]{:S(2)}) copy-start(f32[32,512]{1,0:T(8,128)} %param.6) | copy-start | bytes 196612
  8.0 6.0 %copy-start.4 = (f32[64,512]{1,0:T(8,128)S(1)}, f32[64,512]{1,0:T(8,128)}, u32[]{:S(2)}) copy-start(f32[64,512]{1,0:T(8,128)} %param.5) | copy-start | bytes 393220
  8.0 6.0 %copy-start.3 = (f32[64,2048]{1,0:T(8,128)S(1)}, f32[64,2048]{1,0:T(8,128)}, u32[]{:S(2)}) copy-start(f32[64,2048]{1,0:T(8,128)} %param.7) | copy-start | bytes 1572868
  8.0 408.0 %all-gather.3.cloned.1.call-start = ((), (), s32[]{:S(2)}) async-start(), calls=%async_computation.1 | async-start | bytes 8519680 | tf_op jit(solution)/shard_map/all_gather | solution.py:35
  11.0 4.9 %copy-start.5 = (f32[32,2048]{1,0:T(8,128)S(1)}, f32[32,2048]{1,0:T(8,128)}, u32[]{:S(2)}) copy-start(f32[32,2048]{1,0:T(8,128)} %param.8) | copy-start | bytes 786436
  22.9 1.4 copy-start.1
  27.1 393.7 %all-reduce.2.cloned.1.call-start = ((), (), s32[]{:S(2)}) async-start(), calls=%async_computation | async-start | bytes 1048576 | tf_op jit(solution)/shard_map/psum | solution.py:36
  27.3 1.6 copy-start.2
Sparse Core Ops, SparseCore 0:
  27.2 388.7 all-gather.2
Sparse Core Ops, SparseCore 1:
  31.3 107.8 all-reduce.1
